TPU v7x, 32 devices: a whole 2x2x4 slice. The times are simulated.
32 devices in a mesh: frame: 4 (over y, x), head: 8 (over z, core).
Axes of the slice: x: 2, y: 2, z: 4, core: 2. Of those that a mesh axis runs over, the one named last changes fastest.
Arguments:
- tokens: float32 [8, 1024, 1024], P('frame', 'head'), may hold values from -48 to 48
- qkv_weight: float32 [1024, 3072], replicated
- out_weight: float32 [1024, 1024], replicated, may hold values from -0.1875 to 0.1875
- norm_gain: float32 [1024], replicated, may hold values from 0.1 to 1.9
- proj_weight: float32 [1024, 256], replicated, may hold values from -0.1875 to 0.1875
- up_weight: bfloat16 [256, 4096], replicated, may hold values from -0.375 to 0.375
- conv_weight: bfloat16 [2, 3, 3, 256, 256], replicated, may hold values from -0.125 to 0.125
- conv_bias: float32 [2, 256], replicated, may hold values from -3 to 3
- block_lists: int32 [64, 13], P('frame'), may hold values from 0 to 63, as said below
- block_counts: int32 [64], P('frame'), may hold values from 1 to 13, as said below
Outputs:
- refined: bfloat16 [8, 128, 128, 256], P('frame', 'head')
Inputs may be any that keep to these rules, and one draw needn't show every extreme that they name: `block_lists`: row b names 13 different key blocks and its first entry is block b itself; entries at or after the row's count are padding and are ignored. `block_counts`: some query block in every draw has all 13 entries valid.
All inputs are finite; a program needn't handle non-finite values.
Results may differ from a plain program's by a relative error of at most 0.0057.
Values may be sent and summed in bfloat16 or wider, within the bound.
A program may use at most 128 MiB of HBM per device.

v0:
```python
import math
import jax
import jax.numpy as jnp
from jax import lax
from jax.sharding import PartitionSpec as P

HEADS = 16
GRID = 32
BLOCK = 128
highest = lax.Precision.HIGHEST
eps_norm = 1e-05


def extended_2(block, sides, width):
    for axis, dim in sides:
        count = lax.axis_size(axis)
        forward = [(i, i + 1) for i in range(count - 1)]
        backward = [(target, source) for source, target in forward]
        low = lax.ppermute(
            lax.slice_in_dim(block, block.shape[dim] - width, None, axis=dim), axis, forward
        )
        high = lax.ppermute(lax.slice_in_dim(block, 0, width, axis=dim), axis, backward)
        block = jnp.concatenate([low, block, high], axis=dim)
    return block


def attend_padded(queries, key_values, block_ids, counts, factor):
    groups, slot_total = block_ids.shape
    block_size = queries.shape[1]
    half = queries.shape[3] // 2
    picked = key_values[block_ids]
    picked = picked.reshape((groups, slot_total * block_size) + picked.shape[3:])
    scores = jnp.einsum("gihe,gjhe->ghij", queries, picked, precision=highest) * factor
    slot_of = jnp.arange(slot_total * block_size, dtype=jnp.int32) // block_size
    usable = slot_of[None, :] < counts[:, None]
    scores = jnp.where(usable[:, None, None, :], scores, -jnp.inf)
    row_max = jnp.max(scores, axis=3, keepdims=True)
    weights = jnp.exp(scores - row_max)
    totals = jnp.sum(weights, axis=3)
    blended = jnp.einsum("ghij,gjhe->gihe", weights, picked, precision=highest)
    return blended[:, :, :, half:] / jnp.transpose(totals, (0, 2, 1))[:, :, :, None]


def layer_norm(rows, gain):
    centre = jnp.mean(rows, axis=-1, keepdims=True)
    centred = rows - centre
    spread = jnp.mean(centred * centred, axis=-1, keepdims=True)
    return centred * lax.rsqrt(spread + eps_norm) * gain


def conv_window(padded, weight):
    frames_here, rows_in, cols_in, channels = padded.shape
    rows_out = rows_in - 2
    cols_out = cols_in - 2
    summed = jnp.zeros((frames_here * rows_out * cols_out, weight.shape[-1]), jnp.float32)
    for row_off in range(3):
        for col_off in range(3):
            window = padded[:, row_off : row_off + rows_out, col_off : col_off + cols_out, :]
            summed = summed + jnp.dot(
                window.reshape(-1, channels),
                weight[row_off, col_off],
                preferred_element_type=jnp.float32,
            )
    return summed.reshape(frames_here, rows_out, cols_out, -1)


def pad_columns(image):
    return jnp.pad(image, ((0, 0), (0, 0), (1, 1), (0, 0)))


def on_device(
    tokens,
    qkv_weight,
    out_weight,
    norm_gain,
    proj_weight,
    up_weight,
    conv_weight,
    conv_bias,
    block_lists,
    block_counts,
):
    local_frames, strip_tokens, model_width = tokens.shape
    head_groups = lax.axis_size("head")
    local_heads = HEADS // head_groups
    head_dim = model_width // HEADS
    column_width = local_heads * 3 * head_dim
    frame_tokens = strip_tokens * head_groups
    flat_strip = tokens.reshape(-1, model_width)
    columns = lax.dynamic_slice_in_dim(
        qkv_weight, lax.axis_index("head") * column_width, column_width, 1
    )
    piece = lax.all_gather(tokens, "head", axis=1, tiled=True)
    rows_flat = piece.reshape(-1, model_width)
    result = jnp.dot(rows_flat, columns, precision=highest, preferred_element_type=jnp.float32)
    packed = result.reshape(piece.shape[0], piece.shape[1], column_width)
    local_rows = local_frames * frame_tokens
    packed = packed.reshape(local_rows, local_heads, 3 * head_dim)
    query_mask = (jnp.arange(2 * head_dim, dtype=jnp.int32) < head_dim).astype(jnp.float32)
    queries = (packed[:, :, : 2 * head_dim] * query_mask).reshape(
        -1, BLOCK, local_heads, 2 * head_dim
    )
    own_pairs = packed[:, :, head_dim:].reshape(local_rows, local_heads * 2 * head_dim)
    all_pairs = lax.all_gather(own_pairs, "frame", axis=0, tiled=True)
    all_pairs = all_pairs.reshape(-1, BLOCK, local_heads, 2 * head_dim)
    local_blocks = queries.shape[0]
    group_blocks = math.gcd(local_blocks, max(1, 512 // BLOCK))
    group_count = local_blocks // group_blocks
    factor = head_dim ** (-0.5)
    grouped = (
        queries.reshape(group_count, group_blocks, BLOCK, local_heads, 2 * head_dim),
        block_lists.reshape(group_count, group_blocks, -1),
        block_counts.reshape(group_count, group_blocks),
    )

    def one_group(items):
        return attend_padded(items[0], all_pairs, items[1], items[2], factor)

    attended = lax.map(one_group, grouped)
    attended = attended.reshape(local_frames, head_groups, strip_tokens, local_heads * head_dim)
    attended = lax.all_to_all(attended, "head", split_axis=1, concat_axis=3, tiled=True)
    attended = attended.reshape(-1, model_width)
    stream = flat_strip + jnp.dot(
        attended, out_weight, precision=highest, preferred_element_type=jnp.float32
    )
    normed = layer_norm(stream, norm_gain)
    features = jnp.dot(
        normed, proj_weight, precision=highest, preferred_element_type=jnp.float32
    ).astype(jnp.bfloat16)
    channels = features.shape[1]
    strip_rows = strip_tokens // GRID
    lifted = jnp.dot(features, up_weight, preferred_element_type=jnp.float32).astype(jnp.bfloat16)
    lifted = lifted.reshape(local_frames, strip_rows, GRID, 4, 4, channels)
    upsampled = jnp.transpose(lifted, (0, 1, 3, 2, 4, 5)).reshape(
        local_frames, 4 * strip_rows, 4 * GRID, channels
    )
    activated = jnp.maximum(upsampled, jnp.zeros((), jnp.bfloat16))
    rimmed = extended_2(activated, (("head", 1),), 1)
    first_conv = conv_window(pad_columns(rimmed), conv_weight[0]) + conv_bias[0]
    hidden = jnp.maximum(first_conv, 0.0).astype(jnp.bfloat16)
    extended = extended_2(hidden, (("head", 1),), 1)
    second = conv_window(pad_columns(extended), conv_weight[1]) + conv_bias[1]
    return (upsampled.astype(jnp.float32) + second).astype(jnp.bfloat16)


def solution(mesh):
    in_specs = (
        P("frame", "head", None),
        P(),
        P(),
        P(),
        P(),
        P(),
        P(),
        P(),
        P("frame", None),
        P("frame"),
    )
    out_specs = P("frame", "head", None, None)
    return jax.shard_map(
        on_device, mesh=mesh, in_specs=in_specs, out_specs=out_specs, check_vma=False
    )
```

profile of v0, /device:TPU:1, one launch (start us, length us, event | category | flops | bytes accessed | tf_op | source)
XLA Modules:
  0.0 552.1 jit_solution(14968831860393375033)
XLA Ops:
  7.3 86.2 %all-gather.3.cloned.1.call-done = f32[2,1024,1024]{2,1,0:T(8,128)} async-done(((f32[2,128,1024]{2,1,0:T(8,128)}), f32[2,1024,1024]{2,1,0:T(8,128)}) %all-gather.3.cloned.1.call-update) | async-done | bytes 8388624 | tf_op jit(solution)/shard_map/all_gather | solution.py:93
  93.5 22.6 %fusion.26 = f32[384,2048]{1,0:T(8,128)S(1)} fusion(f32[2048,1024]{1,0:T(8,128)} %bitcast.179, f32[1024,3072]{1,0:T(8,128)} %param.13, s32[]{:T(128)S(6)} %select_n.35), kind=kOutput, calls=%fused_computation.69 | convolution fusion | flops 9663676416 | bytes 13107204 | tf_op jit(solution)/shard_map/dot_general | solution.py:95
  116.1 2.5 fusion.41
  118.6 2.9 copy.60
  122.3 2.9 copy.78
  125.1 3.1 broadcast_multiply_fusion
  128.2 78.9 %all-gather.5.cloned.1.call-done = f32[8192,256]{1,0:T(8,128)} async-done(((f32[2048,256]{1,0:T(8,128)}), f32[8192,256]{1,0:T(8,128)}) %all-gather.5.cloned.1.call-update) | async-done | bytes 8388624 | tf_op jit(solution)/shard_map/all_gather | solution.py:104
  207.1 10.9 %reshape.206 = f32[64,128,2,128]{3,2,1,0:T(2,128)} reshape(f32[8192,256]{1,0:T(8,128)} %all-gather.5.cloned.1.call-done) | data formatting | bytes 16777216 | tf_op jit(solution)/shard_map/reshape | solution.py:105
  218.0 185.2 %while.12 = (s32[]{:T(128)}, f32[4,4,128,2,64]{2,4,3,1,0:T(8,128)S(1)}, s32[4,4,13]{2,1,0:T(4,128)}, f32[64,128,2,128]{3,2,1,0:T(2,128)}, s32[4,4]{1,0:T(4,128)S(1)}, /*index=5*/f32[4,4,128,2,128]{4,2,1,0,3:T(8,128)}, s32[]{:T(128)}) while((s32[]{:T(128)}, f32[4,4,128,2,64]{2,4,3,1,0:T(8,128)S(1)}, s32[4,4,13]{2,1,0:T(4,128)}, ...), condition=%wide.region_3.4_spmd, body=%wide.region_0.3_spmd.sunk | while | flops 5251615744 | bytes 90243968 | solution.py:119
  219.1 14.2 %gather_fusion = f32[52,128,2,128]{3,2,1,0:T(2,128)} fusion(f32[64,128,2,128]{3,2,1,0:T(2,128)} %get-tuple-element.210, s32[1024]{0:T(1024)S(1)} %pad_clamp_fusion.2), kind=kCustom, calls=%fused_computation.clone.1 | custom fusion | bytes 13631696 | tf_op jit(solution)/shard_map/while/body/eval_jaxpr/gather | solution.py:31
  233.2 11.1 %copy.95 = f32[4,1664,2,128]{1,3,2,0:T(8,128)} copy(f32[4,1664,2,128]{3,2,1,0:T(2,128)} %bitcast.165) | data formatting | bytes 13631488 | tf_op jit(solution)/shard_map/while/body/eval_jaxpr/reshape | solution.py:32
  244.4 9.0 %fusion.82 = (f32[4,2,128]{2,1,0:T(2,128)S(1)}, f32[4,2,128,1664]{3,2,1,0:T(8,128)S(1)}) fusion(pred[4,1664]{1,0:T(4,128)(4,1)S(1)} %broadcast_compare_fusion.2, f32[4,1664,2,128]{1,3,2,0:T(8,128)} %copy.95, f32[4,4,128,2,128]{4,2,1,0,3:T(8,128)} %get-tuple-element.212, s32[]{:T(128)} %get-tuple-element.200), kind=kOutput, calls=%fused_computation.3.clone.1 | convolution fusion | flops 2622356480 | bytes 14167040 | tf_op jit(solution)/shard_map/while/body/eval_jaxpr/gihe,gjhe->ghij/dot_general | solution.py:33
  253.5 1.5 fusion.84
  256.4 8.0 %fusion.83 = f32[4,128,2,128]{1,3,2,0:T(8,128)S(1)} fusion(f32[4,1664,2,128]{1,3,2,0:T(8,128)S(1)} %copy-done.2, f32[4,2,128,1664]{3,2,1,0:T(8,128)S(1)} %get-tuple-element.191, f32[4,2,128]{2,1,0:T(2,128)S(1)} %get-tuple-element.192, pred[4,1664]{1,0:T(4,128)(4,1)S(1)} %broadcast_compare_fusion.2), kind=kOutput, calls=%fused_computation.10.clone.1 | convolution fusion | flops 2622357504 | bytes 14166528 | tf_op jit(solution)/shard_map/while/body/eval_jaxpr/ghij,gjhe->gihe/dot_general | solution.py:40
  265.3 14.2 %gather_fusion = f32[52,128,2,128]{3,2,1,0:T(2,128)} fusion(f32[64,128,2,128]{3,2,1,0:T(2,128)} %get-tuple-element.210, s32[1024]{0:T(1024)S(1)} %pad_clamp_fusion.2), kind=kCustom, calls=%fused_computation.clone.1 | custom fusion | bytes 13631696 | tf_op jit(solution)/shard_map/while/body/eval_jaxpr/gather | solution.py:31
  279.4 11.1 %copy.95 = f32[4,1664,2,128]{1,3,2,0:T(8,128)} copy(f32[4,1664,2,128]{3,2,1,0:T(2,128)} %bitcast.165) | data formatting | bytes 13631488 | tf_op jit(solution)/shard_map/while/body/eval_jaxpr/reshape | solution.py:32
  290.6 9.0 %fusion.82 = (f32[4,2,128]{2,1,0:T(2,128)S(1)}, f32[4,2,128,1664]{3,2,1,0:T(8,128)S(1)}) fusion(pred[4,1664]{1,0:T(4,128)(4,1)S(1)} %broadcast_compare_fusion.2, f32[4,1664,2,128]{1,3,2,0:T(8,128)} %copy.95, f32[4,4,128,2,128]{4,2,1,0,3:T(8,128)} %get-tuple-element.212, s32[]{:T(128)} %get-tuple-element.200), kind=kOutput, calls=%fused_computation.3.clone.1 | convolution fusion | flops 2622356480 | bytes 14167040 | tf_op jit(solution)/shard_map/while/body/eval_jaxpr/gihe,gjhe->ghij/dot_general | solution.py:33
  302.6 8.0 %fusion.83 = f32[4,128,2,128]{1,3,2,0:T(8,128)S(1)} fusion(f32[4,1664,2,128]{1,3,2,0:T(8,128)S(1)} %copy-done.2, f32[4,2,128,1664]{3,2,1,0:T(8,128)S(1)} %get-tuple-element.191, f32[4,2,128]{2,1,0:T(2,128)S(1)} %get-tuple-element.192, pred[4,1664]{1,0:T(4,128)(4,1)S(1)} %broadcast_compare_fusion.2), kind=kOutput, calls=%fused_computation.10.clone.1 | convolution fusion | flops 2622357504 | bytes 14166528 | tf_op jit(solution)/shard_map/while/body/eval_jaxpr/ghij,gjhe->gihe/dot_general | solution.py:40
  311.4 14.2 %gather_fusion = f32[52,128,2,128]{3,2,1,0:T(2,128)} fusion(f32[64,128,2,128]{3,2,1,0:T(2,128)} %get-tuple-element.210, s32[1024]{0:T(1024)S(1)} %pad_clamp_fusion.2), kind=kCustom, calls=%fused_computation.clone.1 | custom fusion | bytes 13631696 | tf_op jit(solution)/shard_map/while/body/eval_jaxpr/gather | solution.py:31
  325.6 11.1 %copy.95 = f32[4,1664,2,128]{1,3,2,0:T(8,128)} copy(f32[4,1664,2,128]{3,2,1,0:T(2,128)} %bitcast.165) | data formatting | bytes 13631488 | tf_op jit(solution)/shard_map/while/body/eval_jaxpr/reshape | solution.py:32
  336.8 9.0 %fusion.82 = (f32[4,2,128]{2,1,0:T(2,128)S(1)}, f32[4,2,128,1664]{3,2,1,0:T(8,128)S(1)}) fusion(pred[4,1664]{1,0:T(4,128)(4,1)S(1)} %broadcast_compare_fusion.2, f32[4,1664,2,128]{1,3,2,0:T(8,128)} %copy.95, f32[4,4,128,2,128]{4,2,1,0,3:T(8,128)} %get-tuple-element.212, s32[]{:T(128)} %get-tuple-element.200), kind=kOutput, calls=%fused_computation.3.clone.1 | convolution fusion | flops 2622356480 | bytes 14167040 | tf_op jit(solution)/shard_map/while/body/eval_jaxpr/gihe,gjhe->ghij/dot_general | solution.py:33
  348.7 8.0 %fusion.83 = f32[4,128,2,128]{1,3,2,0:T(8,128)S(1)} fusion(f32[4,1664,2,128]{1,3,2,0:T(8,128)S(1)} %copy-done.2, f32[4,2,128,1664]{3,2,1,0:T(8,128)S(1)} %get-tuple-element.191, f32[4,2,128]{2,1,0:T(2,128)S(1)} %get-tuple-element.192, pred[4,1664]{1,0:T(4,128)(4,1)S(1)} %broadcast_compare_fusion.2), kind=kOutput, calls=%fused_computation.10.clone.1 | convolution fusion | flops 2622357504 | bytes 14166528 | tf_op jit(solution)/shard_map/while/body/eval_jaxpr/ghij,gjhe->gihe/dot_general | solution.py:40
  357.6 14.2 %gather_fusion = f32[52,128,2,128]{3,2,1,0:T(2,128)} fusion(f32[64,128,2,128]{3,2,1,0:T(2,128)} %get-tuple-element.210, s32[1024]{0:T(1024)S(1)} %pad_clamp_fusion.2), kind=kCustom, calls=%fused_computation.clone.1 | custom fusion | bytes 13631696 | tf_op jit(solution)/shard_map/while/body/eval_jaxpr/gather | solution.py:31
  371.7 11.1 %copy.95 = f32[4,1664,2,128]{1,3,2,0:T(8,128)} copy(f32[4,1664,2,128]{3,2,1,0:T(2,128)} %bitcast.165) | data formatting | bytes 13631488 | tf_op jit(solution)/shard_map/while/body/eval_jaxpr/reshape | solution.py:32
  382.9 9.0 %fusion.82 = (f32[4,2,128]{2,1,0:T(2,128)S(1)}, f32[4,2,128,1664]{3,2,1,0:T(8,128)S(1)}) fusion(pred[4,1664]{1,0:T(4,128)(4,1)S(1)} %broadcast_compare_fusion.2, f32[4,1664,2,128]{1,3,2,0:T(8,128)} %copy.95, f32[4,4,128,2,128]{4,2,1,0,3:T(8,128)} %get-tuple-element.212, s32[]{:T(128)} %get-tuple-element.200), kind=kOutput, calls=%fused_computation.3.clone.1 | convolution fusion | flops 2622356480 | bytes 14167040 | tf_op jit(solution)/shard_map/while/body/eval_jaxpr/gihe,gjhe->ghij/dot_general | solution.py:33
  394.9 8.0 %fusion.83 = f32[4,128,2,128]{1,3,2,0:T(8,128)S(1)} fusion(f32[4,1664,2,128]{1,3,2,0:T(8,128)S(1)} %copy-done.2, f32[4,2,128,1664]{3,2,1,0:T(8,128)S(1)} %get-tuple-element.191, f32[4,2,128]{2,1,0:T(2,128)S(1)} %get-tuple-element.192, pred[4,1664]{1,0:T(4,128)(4,1)S(1)} %broadcast_compare_fusion.2), kind=kOutput, calls=%fused_computation.10.clone.1 | convolution fusion | flops 2622357504 | bytes 14166528 | tf_op jit(solution)/shard_map/while/body/eval_jaxpr/ghij,gjhe->gihe/dot_general | solution.py:40
  404.4 5.4 all-to-all-start
  409.9 2.8 slice_bitcast_fusion
  412.7 22.9 %all-to-all-done = f32[2,8,128,128]{3,2,0,1:T(8,128)} async-done(((f32[2,8,128,128]{3,2,0,1:T(8,128)}), f32[2,8,128,128]{3,2,0,1:T(8,128)}, u32[]{:S(2)}, u32[]{:S(2)}) %all-to-all-start) | async-done | bytes 1048608 | tf_op jit(solution)/shard_map/all_to_all | solution.py:121
  435.6 1.9 copy.64
  437.5 6.2 %fusion.47 = (f32[256]{0:T(256)S(1)}, f32[256,1024]{1,0:T(8,128)S(1)}) fusion(f32[256,1024]{1,0:T(8,128)S(1)} %bitcast.194, f32[1024,1024]{1,0:T(8,128)} %param.14, f32[32,8,8,128]{3,2,1,0:T(8,128)S(1)} %bitcast.195), kind=kOutput, calls=%fused_computation.118 | convolution fusion | flops 3221749504 | bytes 7341056 | tf_op jit(solution)/shard_map/dot_general | solution.py:123
  445.2 2.7 broadcast_maximum_fusion
  447.9 4.5 max.34
  452.4 5.0 copy.67
  458.3 1.9 collective-permute-start
  460.2 2.4 collective-permute-start.1
  462.6 2.5 copy.91
  465.1 4.2 max.37
  469.3 5.8 %pad_maximum_fusion.2 = (bf16[2,16,128,256]{3,0,2,1:T(2,128)(2,1)S(1)}, bf16[2,16,128,256]{3,0,2,1:T(2,128)(2,1)S(1)}) fusion(bf16[2,1,128,256]{3,0,2,1:T(2,128)(2,1)S(1)} %collective-permute-done.1, bf16[2,16,128,256]{3,0,2,1:T(2,128)(2,1)S(1)} %bitcast.168, bf16[2,1,128,256]{3,0,2,1:T(2,128)(2,1)S(1)} %collective-permute-done), kind=kLoop, calls=%fused_computation.64 | loop fusion | flops 2097152 | bytes 6553600 | tf_op jit(solution)/shard_map/concatenate | solution.py:23
  475.5 4.2 select_maximum_fusion
  479.7 10.9 %fusion.43 = (bf16[2,16,128,256]{3,0,2,1:T(2,128)(2,1)S(1)}, bf16[2,16,128,256]{3,0,2,1:T(2,128)(2,1)S(1)}, bf16[2,16,128,256]{3,0,2,1:T(2,128)(2,1)S(1)}, bf16[...) fusion(bf16[2,18,130,256]{3,0,2,1:T(2,128)(2,1)S(1)} %select_maxim, ...), kind=kLoop, calls=%fused_computation.114 | loop fusion | bytes 25165824 | tf_op jit(solution)/shard_map/slice | solution.py:58
  504.4 3.1 collective-permute-start.2
  507.6 1.9 collective-permute-start.3
  509.5 6.4 %reshape.229 = f32[2,4,32,4,4,256]{5,4,3,2,1,0:T(4,128)} reshape(bf16[256,4096]{1,0:T(8,128)(2,1)} %get-tuple-element.151) | data formatting | bytes 6291456 | tf_op jit(solution)/shard_map/convert_element_type | solution.py:143
  515.9 5.3 copy.65
  521.2 5.4 reshape.228
  527.7 5.2 fusion.42
  542.5 2.2 add_convert_fusion
  (113 shorter events, 43.7 us)
Async XLA Ops:
  6.5 438.6 %copy-start = (bf16[256,4096]{1,0:T(8,128)(2,1)S(1)}, bf16[256,4096]{1,0:T(8,128)(2,1)}, u32[]{:S(2)}) copy-start(bf16[256,4096]{1,0:T(8,128)(2,1)} %param.17) | copy-start | bytes 6291460
  6.5 86.9 %all-gather.3.cloned.1.call-start = ((), (), s32[]{:S(2)}) async-start(), calls=%async_computation.1 | async-start | bytes 9437184 | tf_op jit(solution)/shard_map/all_gather | solution.py:93
  7.3 199.8 %all-gather.5.cloned.1.call-start = ((), (), s32[]{:S(2)}) async-start(), calls=%async_computation.2 | async-start | bytes 10485760 | tf_op jit(solution)/shard_map/all_gather | solution.py:104
  121.5 0.7 copy-start.13
  253.5 2.9 copy-start.2
  299.6 2.9 copy-start.2
  345.8 2.9 copy-start.2
  392.0 2.9 copy-start.2
  404.4 31.1 %all-to-all-start = ((f32[2,8,128,128]{3,2,0,1:T(8,128)}), f32[2,8,128,128]{3,2,0,1:T(8,128)}, u32[]{:S(2)}, u32[]{:S(2)}) async-start(f32[2,8,128,128]{3,2,0,1:T(8,128)} %copy.63), calls=%async_computation | async-start | bytes 2097152 | tf_op jit(solution)/shard_map/all_to_all | solution.py:121
  435.6 1.9 copy-start.9
  437.5 6.5 %copy-start.10 = (f32[1024,256]{1,0:T(8,128)S(1)}, f32[1024,256]{1,0:T(8,128)}, u32[]{:S(2)}) copy-start(f32[1024,256]{1,0:T(8,128)} %param.16) | copy-start | bytes 3145732
  437.5 6.5 %copy-start.11 = (f32[1024]{0:T(1024)S(1)}, f32[1024]{0:T(1024)}, u32[]{:S(2)}) copy-start(f32[1024]{0:T(1024)} %param.15) | copy-start | bytes 12292
  452.4 10.2 %copy-start.12 = (f32[2,256]{1,0:T(2,128)S(1)}, f32[2,256]{1,0:T(2,128)}, u32[]{:S(2)}) copy-start(f32[2,256]{1,0:T(2,128)} %param.19) | copy-start | bytes 6148
  452.4 10.2 %copy-start.5 = (bf16[2,4,32,4,4,256]{5,4,3,2,1,0:T(4,128)(2,1)S(1)}, bf16[2,4,32,4,4,256]{5,4,3,2,1,0:T(4,128)(2,1)}, u32[]{:S(2)}) copy-start(bf16[2,4,32,4,4,256]{5,4,3,2,1,0:T(4,128)(2,1)} %max.34) | copy-start | bytes 6291460
  458.3 11.0 %collective-permute-start = (bf16[2,1,128,256]{3,0,2,1:T(2,128)(2,1)}, bf16[2,1,128,256]{3,0,2,1:T(2,128)(2,1)S(1)}, u32[]{:S(2)}, u32[]{:S(2)}) collective-permute-start(bf16[2,1,128,256]{3,0,2,1:T(2,128)(2,1)} %get-tuple-element.144), channel_id=1, source_target_pairs={{0,1},{1,2},{2,3},{3,4},{4,5},{5,6},{6,7},{8,9},{9,10},{10,11},{11... | collective-permute-start | bytes 393224 | tf_op jit(solution)/shard_map/ppermute | solution.py:19
  460.2 9.1 %collective-permute-start.1 = (bf16[2,1,128,256]{3,0,2,1:T(2,128)(2,1)}, bf16[2,1,128,256]{3,0,2,1:T(2,128)(2,1)S(1)}, u32[]{:S(2)}, u32[]{:S(2)}) collective-permute-start(bf16[2,1,128,256]{3,0,2,1:T(2,128)(2,1)} %get-tuple-element.145), channel_id=1, source_target_pairs={{1,0},{2,1},{3,2},{4,3},{5,4},{6,5},{7,6},{9,8},{10,9},{11,10},{12... | collective-permute-start | bytes 393224 | tf_op jit(solution)/shard_map/ppermute | solution.py:22
  493.0 1.3 copy-start.8
  496.5 1.6 copy-start.7
  501.8 2.0 copy-start.3
  504.4 22.1 %collective-permute-start.2 = (bf16[2,1,128,256]{3,2,1,0:T(8,128)(2,1)}, bf16[2,1,128,256]{3,2,1,0:T(8,128)(2,1)S(1)}, u32[]{:S(2)}, u32[]{:S(2)}) collective-permute-start(bf16[2,1,128,256]{3,2,1,0:T(8,128)(2,1)} %get-tuple-element.140), channel_id=1, source_target_pairs={{0,1},{1,2},{2,3},{3,4},{4,5},{5,6},{6,7},{8,9},{9,10},{10,11},{11... | collective-permute-start | bytes 393224 | tf_op jit(solution)/shard_map/ppermute | solution.py:19
  507.6 19.0 %collective-permute-start.3 = (bf16[2,1,128,256]{3,2,1,0:T(8,128)(2,1)}, bf16[2,1,128,256]{3,2,1,0:T(8,128)(2,1)S(1)}, u32[]{:S(2)}, u32[]{:S(2)}) collective-permute-start(bf16[2,1,128,256]{3,2,1,0:T(8,128)(2,1)} %get-tuple-element.141), channel_id=1, source_target_pairs={{1,0},{2,1},{3,2},{4,3},{5,4},{6,5},{7,6},{9,8},{10,9},{11,10},{12... | collective-permute-start | bytes 393224 | tf_op jit(solution)/shard_map/ppermute | solution.py:22
  535.3 2.2 copy-start.4
  540.3 2.2 copy-start.6
  542.5 2.2 copy-start.1
Sparse Core Ops, SparseCore 0:
  8.9 84.4 all-gather.2
  121.7 85.3 all-gather.4
where the time goes:
time: 563 us; the launch traced here: 552 us
  local copies, waits for them, and re-layouts  193 us (34%)
  waiting for transfers between devices  189 us (34%)
  matrix products  114 us (20%)
  other arithmetic  26.7 us (5%)
  starting transfers between devices  14.9 us (3%)
  between operations  14.3 us (3%)
    all_gather x1, waiting for transfers between devices, on_device(): piece = lax.all_gather(tokens, 'head', axis=1, tiled=True)  86.2 us
    all_gather x1, waiting for transfers between devices, on_device(): all_pairs = lax.all_gather(own_pairs, 'frame', axis=0, tiled=True)  78.9 us
    gather x4, local copies, waits for them, and re-layouts, attend_padded(): picked = key_values[block_ids]  56.6 us
    reshape x4, local copies, waits for them, and re-layouts, attend_padded(): picked.reshape((groups, slot_total * block_size) + picked.shape[3:])  44.4 us
    dot_general x4, matrix products, attend_padded(): jnp.einsum('gihe,gjhe->ghij', queries, picked, precision=highest) * factor  36.1 us
    dot_general x4, matrix products, attend_padded(): blended = jnp.einsum('ghij,gjhe->gihe', weights, picked, precision=highest)  32.1 us
    all_to_all x1, waiting for transfers between devices, on_device(): lax.all_to_all(attended, 'head', split_axis=1, concat_axis=3, tiled=True)  22.9 us
    dot_general x1, matrix products, on_device(): jnp.dot(rows_flat, columns, precision=highest, preferred_element_type=jnp...  22.6 us
  transfers between devices with their start and end apart: 7, of which 3 were waited for; matrix products, arithmetic and copies ran while one was open for 6% of the time, Pallas kernels for 0%

commit v1 on v0

--- a/solution.py
+++ b/solution.py
@@ -90,7 +90,12 @@
     columns = lax.dynamic_slice_in_dim(
         qkv_weight, lax.axis_index("head") * column_width, column_width, 1
     )
-    piece = lax.all_gather(tokens, "head", axis=1, tiled=True)
+    ring = [tokens]
+    for hop in range(7):
+        ring.append(lax.ppermute(ring[-1], "head", [(dev, (dev + 1) % 8) for dev in range(8)]))
+    piece = jnp.roll(
+        jnp.concatenate(ring[::-1], axis=1), (lax.axis_index("head") + 1) * ring[0].shape[1], axis=1
+    )
     rows_flat = piece.reshape(-1, model_width)
     result = jnp.dot(rows_flat, columns, precision=highest, preferred_element_type=jnp.float32)
     packed = result.reshape(piece.shape[0], piece.shape[1], column_width)

time: 563 us -> 624 us (1.11)
  local copies, waits for them, and re-layouts: 193 us -> 231 us
  starting transfers between devices: 14.9 us -> 32.9 us
    all_gather x1 -> x0, waiting for transfers between devices: 86.2 us -> none  [on_device(): piece = lax.all_gather(tokens, 'head', axis=1, tiled=True)]
    ppermute x0 -> x7, waiting for transfers between devices: none -> 77.1 us  [on_device(): lax.ppermute(ring[-1], 'head', [(dev, (dev + 1) % 8) for dev in range(8)])]
    unnamed x27 -> x64, local copies, waits for them, and re-layouts: 9.38 us -> 39.3 us
    ppermute x0 -> x7, starting transfers between devices: none -> 17.6 us  [on_device(): lax.ppermute(ring[-1], 'head', [(dev, (dev + 1) % 8) for dev in range(8)])]
    all_gather x1, waiting for transfers between devices: 78.9 us -> 95.2 us  [on_device(): all_pairs = lax.all_gather(own_pairs, 'frame', axis=0, tiled=True)]
    dot_general x1, matrix products: 22.6 us -> 10.7 us  [on_device(): jnp.dot(rows_flat, columns, precision=highest, preferred_element_type=jnp...]
    dynamic_slice x0 -> x9, local copies, waits for them, and re-layouts: none -> 9.53 us  [the longest x8 5.18 us: on_device(): attended = lax.map(one_group, grouped)]
    dot_general x4, matrix products: 32.1 us -> 40.7 us  [attend_padded(): blended = jnp.einsum('ghij,gjhe->gihe', weights, picked, precision=highest)]
  transfers between devices with their start and end apart: 7 -> 13, of which waited for: 3 -> 9; matrix products, arithmetic and copies ran while one was open for 6% -> 6% of each run, Pallas kernels for 0% -> 0%
where the time goes in v1:
time: 624 us; the launch traced here: 612 us
  local copies, waits for them, and re-layouts  231 us (37%)
  waiting for transfers between devices  195 us (31%)
  matrix products  110 us (18%)
  starting transfers between devices  32.9 us (5%)
  other arithmetic  28.9 us (5%)
  between operations  14.3 us (2%)
    all_gather x1, waiting for transfers between devices, on_device(): all_pairs = lax.all_gather(own_pairs, 'frame', axis=0, tiled=True)  95.2 us
    ppermute x7, waiting for transfers between devices, on_device(): lax.ppermute(ring[-1], 'head', [(dev, (dev + 1) % 8) for dev in range(8)])  77.1 us
    gather x4, local copies, waits for them, and re-layouts, attend_padded(): picked = key_values[block_ids]  56.7 us
    reshape x4, local copies, waits for them, and re-layouts, attend_padded(): picked.reshape((groups, slot_total * block_size) + picked.shape[3:])  44.3 us
    dot_general x4, matrix products, attend_padded(): blended = jnp.einsum('ghij,gjhe->gihe', weights, picked, precision=highest)  40.7 us
    unnamed x64, local copies, waits for them, and re-layouts  39.3 us
    dot_general x4, matrix products, attend_padded(): jnp.einsum('gihe,gjhe->ghij', queries, picked, precision=highest) * factor  35.7 us
    all_to_all x1, waiting for transfers between devices, on_device(): lax.all_to_all(attended, 'head', split_axis=1, concat_axis=3, tiled=True)  22.4 us
  transfers between devices with their start and end apart: 13, of which 9 were waited for; matrix products, arithmetic and copies ran while one was open for 6% of the time, Pallas kernels for 0%

profile of v1, /device:TPU:1, one launch (start us, length us, event | category | flops | bytes accessed | tf_op | source)
XLA Modules:
  0.0 612.4 jit_solution(16294469498394150457)
XLA Ops:
  6.5 2.7 collective-permute-start
  9.2 12.1 %collective-permute-done = f32[2,128,1024]{2,1,0:T(8,128)S(1)} collective-permute-done((f32[2,128,1024]{2,1,0:T(8,128)}, f32[2,128,1024]{2,1,0:T(8,128)S(1)}, u32[]{:S(2)}, u32[]{:S(2)}) %collective-permute-start) | collective-permute-done | bytes 1048608 | tf_op jit(solution)/shard_map/ppermute | solution.py:95
  23.7 11.7 %collective-permute-done.1 = f32[2,128,1024]{2,1,0:T(8,128)S(1)} collective-permute-done((f32[2,128,1024]{2,1,0:T(8,128)S(1)}, f32[2,128,1024]{2,1,0:T(8,128)S(1)}, u32[]{:S(2)}, u32[]{:S(2)}) %collective-permute-start.1) | collective-permute-done | bytes 1048608 | tf_op jit(solution)/shard_map/ppermute | solution.py:95
  38.8 11.7 %collective-permute-done.2 = f32[2,128,1024]{2,1,0:T(8,128)S(1)} collective-permute-done((f32[2,128,1024]{2,1,0:T(8,128)S(1)}, f32[2,128,1024]{2,1,0:T(8,128)S(1)}, u32[]{:S(2)}, u32[]{:S(2)}) %collective-permute-start.2) | collective-permute-done | bytes 1048608 | tf_op jit(solution)/shard_map/ppermute | solution.py:95
  54.1 11.7 %collective-permute-done.3 = f32[2,128,1024]{2,1,0:T(8,128)S(1)} collective-permute-done((f32[2,128,1024]{2,1,0:T(8,128)S(1)}, f32[2,128,1024]{2,1,0:T(8,128)S(1)}, u32[]{:S(2)}, u32[]{:S(2)}) %collective-permute-start.3) | collective-permute-done | bytes 1048608 | tf_op jit(solution)/shard_map/ppermute | solution.py:95
  69.3 11.7 %collective-permute-done.4 = f32[2,128,1024]{2,1,0:T(8,128)S(1)} collective-permute-done((f32[2,128,1024]{2,1,0:T(8,128)S(1)}, f32[2,128,1024]{2,1,0:T(8,128)S(1)}, u32[]{:S(2)}, u32[]{:S(2)}) %collective-permute-start.4) | collective-permute-done | bytes 1048608 | tf_op jit(solution)/shard_map/ppermute | solution.py:95
  84.5 11.7 %collective-permute-done.5 = f32[2,128,1024]{2,1,0:T(8,128)} collective-permute-done((f32[2,128,1024]{2,1,0:T(8,128)S(1)}, f32[2,128,1024]{2,1,0:T(8,128)}, u32[]{:S(2)}, u32[]{:S(2)}) %collective-permute-start.5) | collective-permute-done | bytes 1048608 | tf_op jit(solution)/shard_map/ppermute | solution.py:95
  101.5 3.1 copy.62
  104.5 6.3 %collective-permute-done.6 = f32[2,128,1024]{2,1,0:T(8,128)} collective-permute-done((f32[2,128,1024]{2,1,0:T(8,128)}, f32[2,128,1024]{2,1,0:T(8,128)}, u32[]{:S(2)}, u32[]{:S(2)}) %collective-permute-start.6) | collective-permute-done | bytes 1048608 | tf_op jit(solution)/shard_map/ppermute | solution.py:95
  133.2 4.3 constant_dynamic-slice_fusion.2
  137.5 10.7 %fusion.45 = f32[2048,2,192]{0,2,1:T(8,128)S(1)} fusion(f32[2048,1024,1]{1,0,2:T(8,128)S(1)} %bitcast.176, f32[2,192,1024]{2,1,0:T(8,128)S(1)} %bitcast.204), kind=kOutput, calls=%fused_computation.133 | convolution fusion | flops 9663676416 | bytes 13107200 | tf_op jit(solution)/shard_map/dot_general | solution.py:100
  150.8 3.6 reshape_reshape.4
  154.5 95.2 %all-gather.2.cloned.1.call-done = f32[8192,256]{0,1:T(8,128)} async-done(((f32[2048,256]{0,1:T(8,128)}), f32[8192,256]{0,1:T(8,128)}) %all-gather.2.cloned.1.call-update) | async-done | bytes 8388624 | tf_op jit(solution)/shard_map/all_gather | solution.py:109
  249.6 8.3 %copy.81 = f32[32,8,64,128]{3,2,1,0:T(8,128)} copy(f32[32,8,64,128]{3,1,2,0:T(8,128)} %bitcast.189) | data formatting | bytes 16777216
  257.9 10.0 %copy.78 = f32[64,128,2,128]{3,2,1,0:T(2,128)} copy(f32[64,128,2,128]{1,0,3,2:T(8,128)} %bitcast.177) | data formatting | bytes 16777216 | tf_op jit(solution)/shard_map/reshape | solution.py:110
  267.9 195.2 %while.12 = (s32[]{:T(128)}, f32[4,4,128,2,64]{2,4,3,1,0:T(8,128)}, s32[4,4,13]{2,1,0:T(4,128)}, f32[64,128,2,128]{3,2,1,0:T(2,128)}, s32[4,4]{1,0:T(4,128)S(1)}, /*index=5*/f32[4,4,128,2,128]{2,1,0,4,3:T(4,128)}, s32[]{:T(128)}) while((s32[]{:T(128)}, f32[4,4,128,2,64]{2,4,3,1,0:T(8,128)}, s32[4,4,13]{2,1,0:T(4,128)}, ...), condition=%wide.region_3.4_spmd, body=%wide.region_0.3_spmd.sunk | while | flops 5251615744 | bytes 65078120 | solution.py:124
  268.7 14.2 %gather_fusion = f32[52,128,2,128]{3,2,1,0:T(2,128)} fusion(f32[64,128,2,128]{3,2,1,0:T(2,128)} %get-tuple-element.216, s32[1024]{0:T(1024)S(1)} %pad_clamp_fusion.2), kind=kCustom, calls=%fused_computation.clone.1 | custom fusion | bytes 13631696 | tf_op jit(solution)/shard_map/while/body/eval_jaxpr/gather | solution.py:31
  282.9 11.1 %copy.93 = f32[4,1664,2,128]{1,3,2,0:T(8,128)} copy(f32[4,1664,2,128]{3,2,1,0:T(2,128)} %bitcast.174) | data formatting | bytes 13631488 | tf_op jit(solution)/shard_map/while/body/eval_jaxpr/reshape | solution.py:32
  295.3 8.9 %fusion.81 = (f32[4,2,128]{2,1,0:T(2,128)S(1)}, f32[4,2,128,1664]{3,2,1,0:T(8,128)S(1)}) fusion(pred[4,1664]{1,0:T(4,128)(4,1)S(1)} %broadcast_compare_fusion.2, f32[4,1664,2,128]{1,3,2,0:T(8,128)} %copy.93, f32[1,4,128,2,128]{4,2,3,1,0:T(8,128)S(1)} %copy.94), kind=kOutput, calls=%fused_computation.3.clone.1 | convolution fusion | flops 2622356480 | bytes 14166528 | tf_op jit(solution)/shard_map/while/body/eval_jaxpr/gihe,gjhe->ghij/dot_general | solution.py:33
  305.7 10.2 %fusion.82 = f32[4,128,2,128]{1,3,2,0:T(8,128)S(1)} fusion(f32[4,1664,2,128]{1,3,2,0:T(8,128)} %copy.93, f32[4,2,128,1664]{3,2,1,0:T(8,128)S(1)} %get-tuple-element.197, f32[4,2,128]{2,1,0:T(2,128)S(1)} %get-tuple-element.198, pred[4,1664]{1,0:T(4,128)(4,1)S(1)} %broadcast_compare_fusion.2), kind=kOutput, calls=%fused_computation.10.clone.1 | convolution fusion | flops 2622357504 | bytes 14166528 | tf_op jit(solution)/shard_map/while/body/eval_jaxpr/ghij,gjhe->gihe/dot_general | solution.py:40
  317.4 14.2 %gather_fusion = f32[52,128,2,128]{3,2,1,0:T(2,128)} fusion(f32[64,128,2,128]{3,2,1,0:T(2,128)} %get-tuple-element.216, s32[1024]{0:T(1024)S(1)} %pad_clamp_fusion.2), kind=kCustom, calls=%fused_computation.clone.1 | custom fusion | bytes 13631696 | tf_op jit(solution)/shard_map/while/body/eval_jaxpr/gather | solution.py:31
  331.6 11.1 %copy.93 = f32[4,1664,2,128]{1,3,2,0:T(8,128)} copy(f32[4,1664,2,128]{3,2,1,0:T(2,128)} %bitcast.174) | data formatting | bytes 13631488 | tf_op jit(solution)/shard_map/while/body/eval_jaxpr/reshape | solution.py:32
  344.1 8.9 %fusion.81 = (f32[4,2,128]{2,1,0:T(2,128)S(1)}, f32[4,2,128,1664]{3,2,1,0:T(8,128)S(1)}) fusion(pred[4,1664]{1,0:T(4,128)(4,1)S(1)} %broadcast_compare_fusion.2, f32[4,1664,2,128]{1,3,2,0:T(8,128)} %copy.93, f32[1,4,128,2,128]{4,2,3,1,0:T(8,128)S(1)} %copy.94), kind=kOutput, calls=%fused_computation.3.clone.1 | convolution fusion | flops 2622356480 | bytes 14166528 | tf_op jit(solution)/shard_map/while/body/eval_jaxpr/gihe,gjhe->ghij/dot_general | solution.py:33
  354.5 10.2 %fusion.82 = f32[4,128,2,128]{1,3,2,0:T(8,128)S(1)} fusion(f32[4,1664,2,128]{1,3,2,0:T(8,128)} %copy.93, f32[4,2,128,1664]{3,2,1,0:T(8,128)S(1)} %get-tuple-element.197, f32[4,2,128]{2,1,0:T(2,128)S(1)} %get-tuple-element.198, pred[4,1664]{1,0:T(4,128)(4,1)S(1)} %broadcast_compare_fusion.2), kind=kOutput, calls=%fused_computation.10.clone.1 | convolution fusion | flops 2622357504 | bytes 14166528 | tf_op jit(solution)/shard_map/while/body/eval_jaxpr/ghij,gjhe->gihe/dot_general | solution.py:40
  366.2 14.2 %gather_fusion = f32[52,128,2,128]{3,2,1,0:T(2,128)} fusion(f32[64,128,2,128]{3,2,1,0:T(2,128)} %get-tuple-element.216, s32[1024]{0:T(1024)S(1)} %pad_clamp_fusion.2), kind=kCustom, calls=%fused_computation.clone.1 | custom fusion | bytes 13631696 | tf_op jit(solution)/shard_map/while/body/eval_jaxpr/gather | solution.py:31
  380.4 11.1 %copy.93 = f32[4,1664,2,128]{1,3,2,0:T(8,128)} copy(f32[4,1664,2,128]{3,2,1,0:T(2,128)} %bitcast.174) | data formatting | bytes 13631488 | tf_op jit(solution)/shard_map/while/body/eval_jaxpr/reshape | solution.py:32
  392.9 8.9 %fusion.81 = (f32[4,2,128]{2,1,0:T(2,128)S(1)}, f32[4,2,128,1664]{3,2,1,0:T(8,128)S(1)}) fusion(pred[4,1664]{1,0:T(4,128)(4,1)S(1)} %broadcast_compare_fusion.2, f32[4,1664,2,128]{1,3,2,0:T(8,128)} %copy.93, f32[1,4,128,2,128]{4,2,3,1,0:T(8,128)S(1)} %copy.94), kind=kOutput, calls=%fused_computation.3.clone.1 | convolution fusion | flops 2622356480 | bytes 14166528 | tf_op jit(solution)/shard_map/while/body/eval_jaxpr/gihe,gjhe->ghij/dot_general | solution.py:33
  403.3 10.2 %fusion.82 = f32[4,128,2,128]{1,3,2,0:T(8,128)S(1)} fusion(f32[4,1664,2,128]{1,3,2,0:T(8,128)} %copy.93, f32[4,2,128,1664]{3,2,1,0:T(8,128)S(1)} %get-tuple-element.197, f32[4,2,128]{2,1,0:T(2,128)S(1)} %get-tuple-element.198, pred[4,1664]{1,0:T(4,128)(4,1)S(1)} %broadcast_compare_fusion.2), kind=kOutput, calls=%fused_computation.10.clone.1 | convolution fusion | flops 2622357504 | bytes 14166528 | tf_op jit(solution)/shard_map/while/body/eval_jaxpr/ghij,gjhe->gihe/dot_general | solution.py:40
  415.0 14.2 %gather_fusion = f32[52,128,2,128]{3,2,1,0:T(2,128)} fusion(f32[64,128,2,128]{3,2,1,0:T(2,128)} %get-tuple-element.216, s32[1024]{0:T(1024)S(1)} %pad_clamp_fusion.2), kind=kCustom, calls=%fused_computation.clone.1 | custom fusion | bytes 13631696 | tf_op jit(solution)/shard_map/while/body/eval_jaxpr/gather | solution.py:31
  429.2 11.1 %copy.93 = f32[4,1664,2,128]{1,3,2,0:T(8,128)} copy(f32[4,1664,2,128]{3,2,1,0:T(2,128)} %bitcast.174) | data formatting | bytes 13631488 | tf_op jit(solution)/shard_map/while/body/eval_jaxpr/reshape | solution.py:32
  441.6 8.9 %fusion.81 = (f32[4,2,128]{2,1,0:T(2,128)S(1)}, f32[4,2,128,1664]{3,2,1,0:T(8,128)S(1)}) fusion(pred[4,1664]{1,0:T(4,128)(4,1)S(1)} %broadcast_compare_fusion.2, f32[4,1664,2,128]{1,3,2,0:T(8,128)} %copy.93, f32[1,4,128,2,128]{4,2,3,1,0:T(8,128)S(1)} %copy.94), kind=kOutput, calls=%fused_computation.3.clone.1 | convolution fusion | flops 2622356480 | bytes 14166528 | tf_op jit(solution)/shard_map/while/body/eval_jaxpr/gihe,gjhe->ghij/dot_general | solution.py:33
  452.0 10.2 %fusion.82 = f32[4,128,2,128]{1,3,2,0:T(8,128)S(1)} fusion(f32[4,1664,2,128]{1,3,2,0:T(8,128)} %copy.93, f32[4,2,128,1664]{3,2,1,0:T(8,128)S(1)} %get-tuple-element.197, f32[4,2,128]{2,1,0:T(2,128)S(1)} %get-tuple-element.198, pred[4,1664]{1,0:T(4,128)(4,1)S(1)} %broadcast_compare_fusion.2), kind=kOutput, calls=%fused_computation.10.clone.1 | convolution fusion | flops 2622357504 | bytes 14166528 | tf_op jit(solution)/shard_map/while/body/eval_jaxpr/ghij,gjhe->gihe/dot_general | solution.py:40
  465.7 5.4 all-to-all-start
  471.1 3.3 slice_bitcast_fusion
  474.4 22.4 %all-to-all-done = f32[2,8,128,128]{3,2,0,1:T(8,128)} async-done(((f32[2,8,128,128]{3,2,0,1:T(8,128)}), f32[2,8,128,128]{3,2,0,1:T(8,128)}, u32[]{:S(2)}, u32[]{:S(2)}) %all-to-all-start) | async-done | bytes 1048608 | tf_op jit(solution)/shard_map/all_to_all | solution.py:126
  498.7 6.2 %fusion.44 = (f32[256]{0:T(256)S(1)}, f32[256,1024]{1,0:T(8,128)S(1)}) fusion(f32[256,1024]{1,0:T(8,128)S(1)} %bitcast.187, f32[1024,1024]{1,0:T(8,128)} %param.14, f32[32,8,8,128]{3,2,1,0:T(8,128)S(1)} %bitcast.205), kind=kOutput, calls=%fused_computation.132 | convolution fusion | flops 3221749504 | bytes 7341056 | tf_op jit(solution)/shard_map/dot_general | solution.py:128
  506.3 2.7 broadcast_maximum_fusion
  509.0 4.5 max.34
  513.5 5.0 copy.69
  525.6 4.1 max.37
  529.7 5.8 pad_maximum_fusion.2
  536.0 4.2 select_maximum_fusion
  540.2 10.9 %fusion.40 = (bf16[2,16,128,256]{3,0,2,1:T(2,128)(2,1)S(1)}, bf16[2,16,128,256]{3,0,2,1:T(2,128)(2,1)S(1)}, bf16[2,16,128,256]{3,0,2,1:T(2,128)(2,1)S(1)}, bf16[...) fusion(bf16[2,18,130,256]{3,0,2,1:T(2,128)(2,1)S(1)} %select_maxim, ...), kind=kLoop, calls=%fused_computation.128 | loop fusion | bytes 25165824 | tf_op jit(solution)/shard_map/slice | solution.py:58
  566.1 3.6 collective-permute-start.9
  569.8 6.4 %reshape.230 = f32[2,4,32,4,4,256]{5,4,3,2,1,0:T(4,128)} reshape(bf16[256,4096]{1,0:T(8,128)(2,1)} %get-tuple-element.157) | data formatting | bytes 6291456 | tf_op jit(solution)/shard_map/convert_element_type | solution.py:148
  576.2 5.3 copy.67
  581.5 5.4 reshape.229
  588.0 5.2 fusion.39
  (164 shorter events, 105.0 us)
Async XLA Ops:
  6.5 499.8 %copy-start = (bf16[256,4096]{1,0:T(8,128)(2,1)S(1)}, bf16[256,4096]{1,0:T(8,128)(2,1)}, u32[]{:S(2)}) copy-start(bf16[256,4096]{1,0:T(8,128)(2,1)} %param.17) | copy-start | bytes 6291460
  6.5 243.1 %all-gather.2.cloned.1.call-start = ((), (), s32[]{:S(2)}) async-start(), calls=%async_computation.1 | async-start | bytes 10485760 | tf_op jit(solution)/shard_map/all_gather | solution.py:109
  6.5 14.7 %collective-permute-start = (f32[2,128,1024]{2,1,0:T(8,128)}, f32[2,128,1024]{2,1,0:T(8,128)S(1)}, u32[]{:S(2)}, u32[]{:S(2)}) collective-permute-start(f32[2,128,1024]{2,1,0:T(8,128)} %param.12), channel_id=1, source_target_pairs={{0,1},{1,2},{2,3},{3,4},{4,5},{5,6},{6,7},{7,0},{8,9},{9,10},{10,1... | collective-permute-start | bytes 3145736 | tf_op jit(solution)/shard_map/ppermute | solution.py:95
  21.3 14.1 %collective-permute-start.1 = (f32[2,128,1024]{2,1,0:T(8,128)S(1)}, f32[2,128,1024]{2,1,0:T(8,128)S(1)}, u32[]{:S(2)}, u32[]{:S(2)}) collective-permute-start(f32[2,128,1024]{2,1,0:T(8,128)S(1)} %collective-permute-done), channel_id=1, source_target_pairs={{0,1},{1,2},{2,3},{3,4},{4,5},{5,6},{6,7},{7,0},{8,9},{9,10},{10,1... | collective-permute-start | bytes 3145736 | tf_op jit(solution)/shard_map/ppermute | solution.py:95
  35.4 1.0 copy-start.12
  36.4 14.2 %collective-permute-start.2 = (f32[2,128,1024]{2,1,0:T(8,128)S(1)}, f32[2,128,1024]{2,1,0:T(8,128)S(1)}, u32[]{:S(2)}, u32[]{:S(2)}) collective-permute-start(f32[2,128,1024]{2,1,0:T(8,128)S(1)} %collective-permute-done.1), channel_id=1, source_target_pairs={{0,1},{1,2},{2,3},{3,4},{4,5},{5,6},{6,7},{7,0},{8,9},{9,10},{10,1... | collective-permute-start | bytes 3145736 | tf_op jit(solution)/shard_map/ppermute | solution.py:95
  50.6 1.0 copy-start.14
  51.6 14.2 %collective-permute-start.3 = (f32[2,128,1024]{2,1,0:T(8,128)S(1)}, f32[2,128,1024]{2,1,0:T(8,128)S(1)}, u32[]{:S(2)}, u32[]{:S(2)}) collective-permute-start(f32[2,128,1024]{2,1,0:T(8,128)S(1)} %collective-permute-done.2), channel_id=1, source_target_pairs={{0,1},{1,2},{2,3},{3,4},{4,5},{5,6},{6,7},{7,0},{8,9},{9,10},{10,1... | collective-permute-start | bytes 3145736 | tf_op jit(solution)/shard_map/ppermute | solution.py:95
  65.8 1.0 copy-start.16
  66.8 14.2 %collective-permute-start.4 = (f32[2,128,1024]{2,1,0:T(8,128)S(1)}, f32[2,128,1024]{2,1,0:T(8,128)S(1)}, u32[]{:S(2)}, u32[]{:S(2)}) collective-permute-start(f32[2,128,1024]{2,1,0:T(8,128)S(1)} %collective-permute-done.3), channel_id=1, source_target_pairs={{0,1},{1,2},{2,3},{3,4},{4,5},{5,6},{6,7},{7,0},{8,9},{9,10},{10,1... | collective-permute-start | bytes 3145736 | tf_op jit(solution)/shard_map/ppermute | solution.py:95
  81.0 1.0 copy-start.18
  82.0 14.2 %collective-permute-start.5 = (f32[2,128,1024]{2,1,0:T(8,128)S(1)}, f32[2,128,1024]{2,1,0:T(8,128)}, u32[]{:S(2)}, u32[]{:S(2)}) collective-permute-start(f32[2,128,1024]{2,1,0:T(8,128)S(1)} %collective-permute-done.4), channel_id=1, source_target_pairs={{0,1},{1,2},{2,3},{3,4},{4,5},{5,6},{6,7},{7,0},{8,9},{9,10},{10,1... | collective-permute-start | bytes 3145736 | tf_op jit(solution)/shard_map/ppermute | solution.py:95
  96.2 14.6 %collective-permute-start.6 = (f32[2,128,1024]{2,1,0:T(8,128)}, f32[2,128,1024]{2,1,0:T(8,128)}, u32[]{:S(2)}, u32[]{:S(2)}) collective-permute-start(f32[2,128,1024]{2,1,0:T(8,128)} %collective-permute-done.5), channel_id=1, source_target_pairs={{0,1},{1,2},{2,3},{3,4},{4,5},{5,6},{6,7},{7,0},{8,9},{9,10},{10,1... | collective-permute-start | bytes 3145736 | tf_op jit(solution)/shard_map/ppermute | solution.py:95
  104.5 11.1 %copy-start.19 = (f32[2,128,1024]{2,1,0:T(8,128)S(1)}, f32[2,128,1024]{2,1,0:T(8,128)}, u32[]{:S(2)}) copy-start(f32[2,128,1024]{2,1,0:T(8,128)} %copy-done.18) | copy-start | bytes 3145732
  113.2 3.5 copy-start.17
  115.6 2.2 copy-start.15
  116.7 2.2 copy-start.13
  118.9 2.1 copy-start.6
  133.2 4.4 copy-start.9
  148.2 2.5 copy-start.23
  465.7 31.1 %all-to-all-start = ((f32[2,8,128,128]{3,2,0,1:T(8,128)}), f32[2,8,128,128]{3,2,0,1:T(8,128)}, u32[]{:S(2)}, u32[]{:S(2)}) async-start(f32[2,8,128,128]{3,2,0,1:T(8,128)} %copy.65), calls=%async_computation | async-start | bytes 2097152 | tf_op jit(solution)/shard_map/all_to_all | solution.py:126
  471.1 27.5 %copy-start.7 = (f32[2,128,1024]{2,1,0:T(8,128)S(1)}, f32[2,128,1024]{2,1,0:T(8,128)}, u32[]{:S(2)}) copy-start(f32[2,128,1024]{2,1,0:T(8,128)} %param.12) | copy-start | bytes 3145732
  498.7 6.5 %copy-start.20 = (f32[1024,256]{1,0:T(8,128)S(1)}, f32[1024,256]{1,0:T(8,128)}, u32[]{:S(2)}) copy-start(f32[1024,256]{1,0:T(8,128)} %param.16) | copy-start | bytes 3145732
  498.7 6.5 %copy-start.21 = (f32[1024]{0:T(1024)S(1)}, f32[1024]{0:T(1024)}, u32[]{:S(2)}) copy-start(f32[1024]{0:T(1024)} %param.15) | copy-start | bytes 12292
  513.5 9.5 %copy-start.22 = (f32[2,256]{1,0:T(2,128)S(1)}, f32[2,256]{1,0:T(2,128)}, u32[]{:S(2)}) copy-start(f32[2,256]{1,0:T(2,128)} %param.19) | copy-start | bytes 6148
  513.5 9.5 %copy-start.4 = (bf16[2,4,32,4,4,256]{5,4,3,2,1,0:T(4,128)(2,1)S(1)}, bf16[2,4,32,4,4,256]{5,4,3,2,1,0:T(4,128)(2,1)}, u32[]{:S(2)}) copy-start(bf16[2,4,32,4,4,256]{5,4,3,2,1,0:T(4,128)(2,1)} %max.34) | copy-start | bytes 6291460
  518.7 11.0 %collective-permute-start.7 = (bf16[2,1,128,256]{3,0,2,1:T(2,128)(2,1)S(1)}, bf16[2,1,128,256]{3,0,2,1:T(2,128)(2,1)S(1)}, u32[]{:S(2)}, u32[]{:S(2)}) collective-permute-start(bf16[2,1,128,256]{3,0,2,1:T(2,128)(2,1)S(1)} %get-tuple-element.150), channel_id=1, source_target_pairs={{0,1},{1,2},{2,3},{3,4},{4,5},{5,6},{6,7},{8,9},{9,10},{10,11},{11... | collective-permute-start | bytes 393224 | tf_op jit(solution)/shard_map/ppermute | solution.py:19
  520.6 9.1 %collective-permute-start.8 = (bf16[2,1,128,256]{3,0,2,1:T(2,128)(2,1)S(1)}, bf16[2,1,128,256]{3,0,2,1:T(2,128)(2,1)S(1)}, u32[]{:S(2)}, u32[]{:S(2)}) collective-permute-start(bf16[2,1,128,256]{3,0,2,1:T(2,128)(2,1)S(1)} %get-tuple-element.151), channel_id=1, source_target_pairs={{1,0},{2,1},{3,2},{4,3},{5,4},{6,5},{7,6},{9,8},{10,9},{11,10},{12... | collective-permute-start | bytes 393224 | tf_op jit(solution)/shard_map/ppermute | solution.py:22
  553.5 1.3 copy-start.11
  557.0 1.6 copy-start.8
  562.2 2.0 copy-start.2
  564.2 22.7 %collective-permute-start.10 = (bf16[2,1,128,256]{3,2,1,0:T(8,128)(2,1)S(1)}, bf16[2,1,128,256]{3,2,1,0:T(8,128)(2,1)S(1)}, u32[]{:S(2)}, u32[]{:S(2)}) collective-permute-start(bf16[2,1,128,256]{3,2,1,0:T(8,128)(2,1)S(1)} %get-tuple-element.147), channel_id=1, source_target_pairs={{1,0},{2,1},{3,2},{4,3},{5,4},{6,5},{7,6},{9,8},{10,9},{11,10},{12... | collective-permute-start | bytes 393224 | tf_op jit(solution)/shard_map/ppermute | solution.py:22
  566.1 20.8 %collective-permute-start.9 = (bf16[2,1,128,256]{3,2,1,0:T(8,128)(2,1)S(1)}, bf16[2,1,128,256]{3,2,1,0:T(8,128)(2,1)S(1)}, u32[]{:S(2)}, u32[]{:S(2)}) collective-permute-start(bf16[2,1,128,256]{3,2,1,0:T(8,128)(2,1)S(1)} %get-tuple-element.146), channel_id=1, source_target_pairs={{0,1},{1,2},{2,3},{3,4},{4,5},{5,6},{6,7},{8,9},{9,10},{10,11},{11... | collective-permute-start | bytes 393224 | tf_op jit(solution)/shard_map/ppermute | solution.py:19
  588.0 5.2 copy-start.10
  595.6 2.2 copy-start.3
  600.7 2.2 copy-start.5
  602.9 2.2 copy-start.1
Sparse Core Ops, SparseCore 0:
  150.8 98.7 all-gather.1
